TPU v7x, 32 devices: a whole 2x2x4 slice. The times are simulated.
32 devices in a mesh: doc: 8 (over y, x, core), seq: 4 (over z).
Axes of the slice: x: 2, y: 2, z: 4, core: 2. Of those that a mesh axis runs over, the one named last changes fastest.
Arguments:
- images: bfloat16 [8, 4, 128, 8192], P('doc', None, None, 'seq'), may hold values from -6 to 6
- kv_weight: bfloat16 [1024, 8192], P('doc', 'seq'), may hold values from -0.0625 to 0.0625
- q_gain: float32 [128], replicated, may hold values from 0.1 to 1.9
- k_gain: float32 [128], replicated, may hold values from 0.1 to 1.9
- queries: bfloat16 [8, 512, 4096], P('doc', 'seq'), may hold values from -6 to 6
- cotangent: bfloat16 [8, 512, 4096], P('doc', 'seq'), may hold values from -6 to 6
- tile_count: int32 [8], replicated, may hold values from 1 to 4, as said below
- tile_target: int32 [8, 4], replicated, may hold values from 0 to 8, as said below
- tile_source: int32 [8, 4], replicated, may hold values from 0 to 8, as said below
- text_length: int32 [8], replicated, may hold values from 64 to 512, as said below
Outputs:
- attn_out: bfloat16 [8, 512, 4096], P('doc', 'seq')
- kv_weight_grad: float32 [1024, 8192], P('doc', 'seq')
Inputs may be any that keep to these rules, and one draw needn't show every extreme that they name: `tile_count`: some document has 4 tiles and some has 1. `tile_target`: 8 marks an empty slot. The tile in slot k of an encoder device is tile k of its document; no encoder device holds two tiles of one document. Agrees with tile_source and tile_count. `tile_source`: 8 for k at or beyond the document's tile count; otherwise the encoder device that holds tile k in its slot k. `text_length`: live rows come first; some document has all 512 rows live.
All inputs are finite; a program needn't handle non-finite values.
Results may differ from a plain program's by a relative error of at most 0.03.
Values may be sent and summed in bfloat16 or wider, within the bound.
No kernel may reach another device: no remote copies, remote signals or barrier semaphores. Data moves between devices by JAX's collectives and lax.ppermute only.
A program may use at most 64 MiB of HBM per device.

v0:
```python
import math
import jax
import jax.numpy as jnp
from jax import lax
from jax.sharding import PartitionSpec as P

EPS = 1e-05


def cross_core(kv_tiles, query_rows, grad_rows, q_gain, k_gain, key_live, row_live):
    key_width = kv_tiles.shape[-1] // 2
    head_dim = q_gain.shape[0]
    kv_heads = key_width // head_dim
    token_rows = query_rows.shape[0]
    q_heads = query_rows.shape[1] // head_dim
    group_size = q_heads // kv_heads
    inv_root = 1.0 / math.sqrt(head_dim)
    key_raw = kv_tiles[:, :key_width].reshape(-1, kv_heads, head_dim).astype(jnp.float32)
    values = kv_tiles[:, key_width:].reshape(-1, kv_heads, head_dim)
    key_scale = lax.rsqrt(jnp.mean(key_raw * key_raw, axis=-1, keepdims=True) + EPS)
    key_normed = (key_raw * key_scale * k_gain).astype(jnp.bfloat16)
    query_raw = query_rows.reshape(token_rows, kv_heads, group_size, head_dim).astype(jnp.float32)
    query_scale = lax.rsqrt(jnp.mean(query_raw * query_raw, axis=-1, keepdims=True) + EPS)
    query_normed = (query_raw * query_scale * q_gain).astype(jnp.bfloat16)
    row_mask = row_live[:, None, None, None]
    grad_live = grad_rows.reshape(token_rows, kv_heads, group_size, head_dim) * row_mask.astype(
        jnp.bfloat16
    )

    def one_head(items):
        key_head, value_head, query_head, grad_head = items
        scores = (
            jnp.einsum("tgd,ld->tgl", query_head, key_head, preferred_element_type=jnp.float32)
            * inv_root
        )
        expd = jnp.exp(scores) * key_live
        attend = expd / jnp.sum(expd, axis=-1, keepdims=True)
        attend_low = attend.astype(jnp.bfloat16)
        mixed = jnp.einsum(
            "tgl,ld->tgd", attend_low, value_head, preferred_element_type=jnp.float32
        )
        mixed_low = (mixed * row_live[:, None, None]).astype(jnp.bfloat16)
        grad_attend = jnp.einsum(
            "tgd,ld->tgl", grad_head, value_head, preferred_element_type=jnp.float32
        )
        grad_scores = attend * (grad_attend - jnp.sum(attend * grad_attend, axis=-1, keepdims=True))
        grad_low = (grad_scores * inv_root).astype(jnp.bfloat16)
        grad_keyn = jnp.einsum(
            "tgl,tgd->ld", grad_low, query_head, preferred_element_type=jnp.float32
        )
        grad_values = jnp.einsum(
            "tgl,tgd->ld", attend_low, grad_head, preferred_element_type=jnp.float32
        )
        return (mixed_low, grad_keyn, grad_values)

    head_items = (
        jnp.moveaxis(key_normed, 1, 0),
        jnp.moveaxis(values, 1, 0),
        jnp.moveaxis(query_normed, 1, 0),
        jnp.moveaxis(grad_live, 1, 0),
    )
    mixed_heads, keyn_heads, value_heads = lax.map(one_head, head_items)
    attn_rows = jnp.moveaxis(mixed_heads, 0, 1).reshape(token_rows, -1)
    grad_keyn = jnp.moveaxis(keyn_heads, 0, 1)
    grad_values = jnp.moveaxis(value_heads, 0, 1)
    weighted = grad_keyn * k_gain
    cubed = key_scale * key_scale * key_scale
    grad_keys = key_scale * weighted - key_raw * cubed * jnp.mean(
        weighted * key_raw, axis=-1, keepdims=True
    )
    grad_kv = jnp.concatenate(
        [grad_keys.reshape(-1, key_width), grad_values.reshape(-1, key_width)], axis=-1
    )
    return (attn_rows, grad_kv)


def per_device(
    images,
    kv_weight,
    q_gain,
    k_gain,
    queries,
    cotangent,
    tile_count,
    tile_target,
    tile_source,
    text_length,
):
    n_doc = lax.axis_size("doc")
    n_seq = lax.axis_size("seq")
    doc_at = lax.axis_index("doc")
    seq_at = lax.axis_index("seq")
    slots = images.shape[1]
    tile_rows = images.shape[2]
    part_rows = tile_rows // n_seq
    own_cols = images[0].reshape(slots * tile_rows, images.shape[3])
    partial_value = lax.dot_general(
        own_cols,
        lax.all_gather(kv_weight, "doc", axis=0, tiled=True),
        (((1,), (1,)), ((), ())),
        preferred_element_type=jnp.float32,
    )
    width = partial_value.shape[1]
    partial_value = partial_value.reshape(slots, tile_rows, width)
    summed = lax.psum(partial_value.astype(jnp.bfloat16), "seq").astype(jnp.float32)
    own_share = lax.dynamic_slice_in_dim(summed, seq_at * part_rows, part_rows, 1)
    kv_own = own_share.astype(jnp.bfloat16)
    doc_ids = jnp.arange(n_doc, dtype=jnp.int32)
    slot_ids = jnp.arange(slots, dtype=jnp.int32)
    targets = tile_target[doc_at]
    send_map = (targets[None, :] == doc_ids[:, None]).astype(jnp.bfloat16)
    outgoing = jnp.einsum(
        "ds,src->drc", send_map, kv_own, preferred_element_type=jnp.float32
    ).astype(jnp.bfloat16)
    incoming = lax.all_to_all(outgoing, "doc", split_axis=0, concat_axis=0, tiled=True)
    tiles_here = tile_count[doc_at]
    sources = tile_source[doc_at]
    live_slot = slot_ids < tiles_here
    pick_map = ((sources[:, None] == doc_ids[None, :]) & live_slot[:, None]).astype(jnp.bfloat16)
    kv_part = jnp.einsum(
        "se,erc->src", pick_map, incoming, preferred_element_type=jnp.float32
    ).astype(jnp.bfloat16)
    kv_full = lax.all_gather(kv_part, "seq", axis=1, tiled=True)
    token_rows = queries.shape[1]
    key_live = (jnp.arange(slots * tile_rows, dtype=jnp.int32) // tile_rows < tiles_here).astype(
        jnp.float32
    )
    row_index = seq_at * token_rows + jnp.arange(token_rows, dtype=jnp.int32)
    row_live = (row_index < text_length[doc_at]).astype(jnp.float32)
    attn_rows, grad_kv = cross_core(
        kv_full.reshape(slots * tile_rows, width),
        queries[0],
        cotangent[0],
        q_gain,
        k_gain,
        key_live,
        row_live,
    )
    attn_out = attn_rows[None]
    grad_kv = grad_kv.reshape(slots, tile_rows, width)
    grad_sum = lax.psum(grad_kv.astype(jnp.bfloat16), "seq").astype(jnp.float32)
    grad_share = lax.dynamic_slice_in_dim(grad_sum, seq_at * part_rows, part_rows, 1)
    grad_own = grad_share.astype(jnp.bfloat16)
    back_out = jnp.einsum(
        "se,src->erc", pick_map, grad_own, preferred_element_type=jnp.float32
    ).astype(jnp.bfloat16)
    back_in = lax.all_to_all(back_out, "doc", split_axis=0, concat_axis=0, tiled=True)
    returned = jnp.einsum(
        "ds,drc->src", send_map, back_in, preferred_element_type=jnp.float32
    ).astype(jnp.bfloat16)
    grad_full = lax.all_gather(returned, "seq", axis=1, tiled=True)
    grad_flat = grad_full.reshape(slots * tile_rows, width)
    rows_each = width // n_doc
    weight_part = lax.dot_general(
        grad_flat, own_cols, (((0,), (0,)), ((), ())), preferred_element_type=jnp.float32
    )
    weight_sum = lax.psum(weight_part.astype(jnp.bfloat16), "doc").astype(jnp.float32)
    weight_grad = lax.dynamic_slice_in_dim(weight_sum, doc_at * rows_each, rows_each, 0)
    return (attn_out, weight_grad)


def solution(mesh):
    return jax.shard_map(
        per_device,
        mesh=mesh,
        in_specs=(
            P("doc", None, None, "seq"),
            P("doc", "seq"),
            P(),
            P(),
            P("doc", "seq", None),
            P("doc", "seq", None),
            P(),
            P(),
            P(),
            P(),
        ),
        out_specs=(P("doc", "seq", None), P("doc", "seq")),
        check_vma=False,
    )
```

profile of v0, /device:TPU:0, one launch (start us, length us, event | category | flops | bytes accessed | tf_op | source)
XLA Modules:
  0.0 441.7 jit_solution(6251067855293527332)
XLA Ops:
  7.2 0.7 all-gather.4.cloned.1.call-update
  8.0 41.2 %all-gather.4.cloned.1.call-done = bf16[1024,2048]{1,0:T(8,128)(2,1)} async-done(((bf16[128,2048]{1,0:T(8,128)(2,1)}), bf16[1024,2048]{1,0:T(8,128)(2,1)}) %all-gather.4.cloned.1.call-update) | async-done | bytes 4194320 | tf_op jit(solution)/shard_map/all_gather | solution.py:99
  49.2 5.5 %fusion.64 = bf16[4,128,1024]{2,1,0:T(8,128)(2,1)} fusion(bf16[1024,2048]{1,0:T(8,128)(2,1)} %all-gather.4.cloned.1.call-done, bf16[1,4,128,2048]{3,2,1,0:T(8,128)(2,1)S(1)} %copy-done), kind=kOutput, calls=%fused_computation.63 | convolution fusion | flops 2148007936 | bytes 7340032 | tf_op jit(solution)/shard_map/dot_general | solution.py:97
  55.0 51.8 %all-reduce.4.cloned.1.call-done = bf16[4,128,1024]{2,1,0:T(8,128)(2,1)} async-done(((bf16[4,128,1024]{2,1,0:T(8,128)(2,1)}), bf16[4,128,1024]{2,1,0:T(8,128)(2,1)}) %all-reduce.4.cloned.1.call-update) | async-done | bytes 1048592 | tf_op jit(solution)/shard_map/psum | solution.py:105
  106.8 1.0 convert_convert_fusion.1
  108.2 1.1 copy.35
  109.3 3.7 all-to-all-start
  113.8 0.6 iota_compare_fusion.2
  114.5 8.2 %all-to-all-done = bf16[8,32,1024]{2,1,0:T(8,128)(2,1)S(1)} async-done(((bf16[8,32,1024]{2,1,0:T(8,128)(2,1)}), bf16[8,32,1024]{2,1,0:T(8,128)(2,1)S(1)}, u32[]{:S(2)}, u32[]{:S(2)}) %all-to-all-start) | async-done | bytes 524320 | tf_op jit(solution)/shard_map/all_to_all | solution.py:115
  122.7 1.1 convolution_convert_fusion.4
  124.1 0.7 dynamic_slice.39
  124.8 2.3 copy.40
  127.0 1.6 copy.33
  128.7 0.6 fusion.86
  129.6 2.3 multiply_bitcast_fusion
  131.9 1.4 fusion.69
  133.3 16.2 %all-gather.6.cloned.1.call-done = bf16[4,128,1024]{2,0,1:T(4,128)(2,1)} async-done(((bf16[4,32,1024]{2,0,1:T(4,128)(2,1)}), bf16[4,128,1024]{2,0,1:T(4,128)(2,1)}) %all-gather.6.cloned.1.call-update) | async-done | bytes 1048592 | tf_op jit(solution)/shard_map/all_gather | solution.py:123
  149.5 1.5 copy.37
  151.0 1.3 fusion.89
  152.3 1.6 copy.38
  154.0 2.1 copy.39
  156.1 1.0 fusion.73
  157.1 87.8 %while.15 = (s32[]{:T(128)}, bf16[4,128,8,128]{3,1,2,0:T(8,128)(2,1)}, f32[4,512,128]{1,2,0:T(8,128)}, bf16[4,512,128]{2,1,0:T(8,128)(2,1)}, bf16[4,128,8,128]{1...) while((s32[]{:T(128)}, ...), condition=%wide.region_6.7_spmd.clone, body=%wide.region_3.6_spmd.clone.sunk | while | flops 682891136 | bytes 27433116 | solution.py:62
  157.1 0.6 fusion.114
  157.7 2.8 fusion.115
  160.5 2.7 fusion.117
  163.2 9.8 %fusion.118 = f32[4,512,128]{1,2,0:T(8,128)} fusion(f32[4,512,128]{1,2,0:T(8,128)} %get-tuple-element.222, s32[]{:T(128)} %get-tuple-element.220, f32[128,8,512]{2,0,1:T(8,128)} %fusion.117, bf16[4,128,8,128]{1,3,2,0:T(8,128)(2,1)} %get-tuple-element.236, f32[128,8,512]{2,0,1:T(8,128)} %get-tuple-element.206, f32[128,8]{0,1:T(8,128)S(1)} %get-tuple-element.207, ...), kind=kOutput, calls=%fused_computation.13.clone.1 | convolution fusion | flops 139986432 | bytes 8926208 | tf_op jit(solution)/shard_map/while/body/eval_jaxpr/tgl,tgd->ld/dot_general | solution.py:48
  173.0 3.1 fusion.119
  176.1 0.6 compare_convert_fusion.3
  176.8 2.2 fusion.116
  179.0 0.6 fusion.114
  179.6 2.8 fusion.115
  182.4 2.7 fusion.117
  185.2 9.8 %fusion.118 = f32[4,512,128]{1,2,0:T(8,128)} fusion(f32[4,512,128]{1,2,0:T(8,128)} %get-tuple-element.222, s32[]{:T(128)} %get-tuple-element.220, f32[128,8,512]{2,0,1:T(8,128)} %fusion.117, bf16[4,128,8,128]{1,3,2,0:T(8,128)(2,1)} %get-tuple-element.236, f32[128,8,512]{2,0,1:T(8,128)} %get-tuple-element.206, f32[128,8]{0,1:T(8,128)S(1)} %get-tuple-element.207, ...), kind=kOutput, calls=%fused_computation.13.clone.1 | convolution fusion | flops 139986432 | bytes 8926208 | tf_op jit(solution)/shard_map/while/body/eval_jaxpr/tgl,tgd->ld/dot_general | solution.py:48
  195.0 3.1 fusion.119
  198.7 2.2 fusion.116
  200.9 0.6 fusion.114
  201.6 2.8 fusion.115
  204.4 2.7 fusion.117
  207.1 9.8 %fusion.118 = f32[4,512,128]{1,2,0:T(8,128)} fusion(f32[4,512,128]{1,2,0:T(8,128)} %get-tuple-element.222, s32[]{:T(128)} %get-tuple-element.220, f32[128,8,512]{2,0,1:T(8,128)} %fusion.117, bf16[4,128,8,128]{1,3,2,0:T(8,128)(2,1)} %get-tuple-element.236, f32[128,8,512]{2,0,1:T(8,128)} %get-tuple-element.206, f32[128,8]{0,1:T(8,128)S(1)} %get-tuple-element.207, ...), kind=kOutput, calls=%fused_computation.13.clone.1 | convolution fusion | flops 139986432 | bytes 8926208 | tf_op jit(solution)/shard_map/while/body/eval_jaxpr/tgl,tgd->ld/dot_general | solution.py:48
  216.9 3.1 fusion.119
  220.7 2.2 fusion.116
  222.9 0.6 fusion.114
  223.5 2.8 fusion.115
  226.3 2.7 fusion.117
  229.0 9.8 %fusion.118 = f32[4,512,128]{1,2,0:T(8,128)} fusion(f32[4,512,128]{1,2,0:T(8,128)} %get-tuple-element.222, s32[]{:T(128)} %get-tuple-element.220, f32[128,8,512]{2,0,1:T(8,128)} %fusion.117, bf16[4,128,8,128]{1,3,2,0:T(8,128)(2,1)} %get-tuple-element.236, f32[128,8,512]{2,0,1:T(8,128)} %get-tuple-element.206, f32[128,8]{0,1:T(8,128)S(1)} %get-tuple-element.207, ...), kind=kOutput, calls=%fused_computation.13.clone.1 | convolution fusion | flops 139986432 | bytes 8926208 | tf_op jit(solution)/shard_map/while/body/eval_jaxpr/tgl,tgd->ld/dot_general | solution.py:48
  238.9 3.1 fusion.119
  242.6 2.2 fusion.116
  244.8 1.5 fusion.72
  246.4 1.1 fusion.71
  247.5 1.2 reshape.87
  248.7 1.2 copy.49
  250.9 2.5 pad_maximum_fusion
  253.5 51.4 %all-reduce.6.cloned.1.call-done = bf16[4,128,1024]{2,0,1:T(4,128)(2,1)} async-done(((bf16[4,128,1024]{2,0,1:T(4,128)(2,1)}), bf16[4,128,1024]{2,0,1:T(4,128)(2,1)}) %all-reduce.6.cloned.1.call-update) | async-done | bytes 1048592 | tf_op jit(solution)/shard_map/psum | solution.py:141
  304.9 1.4 convolution_convert_fusion.1
  306.5 13.2 %all_to_all.10 = bf16[8,32,1024]{2,1,0:T(8,128)(2,1)S(1)} all-to-all(bf16[8,32,1024]{2,1,0:T(8,128)(2,1)S(1)} %copy.51), channel_id=1, replica_groups=mesh['doc'=8,'seq'=4] {'doc'}, dimensions={0} | all-to-all | bytes 1048576 | tf_op jit(solution)/shard_map/all_to_all | solution.py:147
  319.7 1.1 convolution_convert_fusion.3
  321.1 25.3 %all-gather.8.cloned.1.call-done = bf16[4,128,1024]{2,0,1:T(4,128)(2,1)} async-done(((bf16[4,32,1024]{2,0,1:T(4,128)(2,1)}), bf16[4,128,1024]{2,0,1:T(4,128)(2,1)}) %all-gather.8.cloned.1.call-update) | async-done | bytes 1048592 | tf_op jit(solution)/shard_map/all_gather | solution.py:151
  346.5 1.5 copy.53
  348.0 4.4 convolution_convert_fusion
  352.4 1.9 copy.45
  354.3 1.3 broadcast_in_dim_reshape.3
  355.6 77.2 %all-reduce.8.cloned.1.call-done = bf16[1024,2048]{1,0:T(8,128)(2,1)} async-done(((bf16[1024,2048]{1,0:T(8,128)(2,1)}), bf16[1024,2048]{1,0:T(8,128)(2,1)}) %all-reduce.8.cloned.1.call-update) | async-done | bytes 4194320 | tf_op jit(solution)/shard_map/psum | solution.py:157
  432.7 2.1 dynamic-slice_convert_fusion
  (56 shorter events, 5.8 us)
Async XLA Ops:
  7.2 42.1 %copy-start = (bf16[1,4,128,2048]{3,2,1,0:T(8,128)(2,1)S(1)}, bf16[1,4,128,2048]{3,2,1,0:T(8,128)(2,1)}, u32[]{:S(2)}) copy-start(bf16[1,4,128,2048]{3,2,1,0:T(8,128)(2,1)} %param.12) | copy-start | bytes 6291460
  7.2 42.0 %all-gather.4.cloned.1.call-start = ((), (), s32[]{:S(2)}) async-start(), calls=%async_computation.2 | async-start | bytes 4718592 | tf_op jit(solution)/shard_map/all_gather | solution.py:99
  7.9 46.9 %copy-start.5 = (s32[8,4]{0,1:T(4,128)S(1)}, s32[8,4]{0,1:T(4,128)}, u32[]{:S(2)}) copy-start(s32[8,4]{0,1:T(4,128)} %param.19) | copy-start | bytes 388
  7.9 98.9 %all-reduce.4.cloned.1.call-start = ((), (), s32[]{:S(2)}) async-start(), calls=%async_computation.3 | async-start | bytes 2097152 | tf_op jit(solution)/shard_map/psum | solution.py:105
  54.7 58.3 %copy-start.8 = (s32[8]{0:T(128)S(1)}, s32[8]{0:T(128)}, u32[]{:S(2)}) copy-start(s32[8]{0:T(128)} %param.18) | copy-start | bytes 100
  54.7 58.9 %copy-start.6 = (s32[8,4]{0,1:T(4,128)S(1)}, s32[8,4]{0,1:T(4,128)}, u32[]{:S(2)}) copy-start(s32[8,4]{0,1:T(4,128)} %param.20) | copy-start | bytes 388
  107.8 16.3 %copy-start.9 = (s32[8]{0:T(128)S(1)}, s32[8]{0:T(128)}, u32[]{:S(2)}) copy-start(s32[8]{0:T(128)} %param.21) | copy-start | bytes 100
  109.3 13.4 %all-to-all-start = ((bf16[8,32,1024]{2,1,0:T(8,128)(2,1)}), bf16[8,32,1024]{2,1,0:T(8,128)(2,1)S(1)}, u32[]{:S(2)}, u32[]{:S(2)}) async-start(bf16[8,32,1024]{2,1,0:T(8,128)(2,1)} %copy.35), calls=%async_computation | async-start | bytes 1048576 | tf_op jit(solution)/shard_map/all_to_all | solution.py:115
  113.0 36.5 %all-gather.6.cloned.1.call-start = ((), (), s32[]{:S(2)}) async-start(), calls=%async_computation.4 | async-start | bytes 1310720 | tf_op jit(solution)/shard_map/all_gather | solution.py:123
  123.9 181.0 %all-reduce.6.cloned.1.call-start = ((), (), s32[]{:S(2)}) async-start(), calls=%async_computation.5 | async-start | bytes 2097152 | tf_op jit(solution)/shard_map/psum | solution.py:141
  128.7 3.2 copy-start.7
  152.3 3.8 copy-start.4
  173.0 3.7 copy-start.1
  195.0 3.7 copy-start.1
  216.9 3.7 copy-start.1
  238.9 3.7 copy-start.1
  244.8 1.5 copy-start.2
  247.5 2.4 copy-start.3
  253.4 93.0 %all-gather.8.cloned.1.call-start = ((), (), s32[]{:S(2)}) async-start(), calls=%async_computation.6 | async-start | bytes 1310720 | tf_op jit(solution)/shard_map/all_gather | solution.py:151
  320.9 111.9 %all-reduce.8.cloned.1.call-start = ((), (), s32[]{:S(2)}) async-start(), calls=%async_computation.7 | async-start | bytes 8388608 | tf_op jit(solution)/shard_map/psum | solution.py:157
Sparse Core Ops, SparseCore 0:
  9.9 39.2 all-gather.3
  54.9 51.8 all-reduce.3
  124.0 25.4 all-gather.5
  253.6 51.2 all-reduce.5
  321.0 25.4 all-gather.7
  352.5 80.1 all-reduce.7
where the time goes:
time: 443 us; the launch traced here: 442 us
  waiting for transfers between devices  272 us (61%)
  matrix products  96.6 us (22%)
  other arithmetic  20.8 us (5%)
  local copies, waits for them, and re-layouts  20.3 us (5%)
  between operations  14.3 us (3%)
  blocking collectives  13.2 us (3%)
    psum x1, waiting for transfers between devices, per_device(): lax.psum(weight_part.astype(jnp.bfloat16), 'doc').astype(jnp.float32)  77.2 us
    psum x1, waiting for transfers between devices, per_device(): lax.psum(partial_value.astype(jnp.bfloat16), 'seq').astype(jnp.float32)  51.8 us
    psum x1, waiting for transfers between devices, per_device(): grad_sum = lax.psum(grad_kv.astype(jnp.bfloat16), 'seq').astype(jnp.float32)  51.4 us
    all_gather x1, waiting for transfers between devices, per_device(): lax.all_gather(kv_weight, 'doc', axis=0, tiled=True)  41.2 us
    dot_general x4, matrix products, one_head(): jnp.einsum('tgl,tgd->ld', grad_low, query_head, preferred_element_type=jn...  39.3 us
    all_gather x1, waiting for transfers between devices, per_device(): grad_full = lax.all_gather(returned, 'seq', axis=1, tiled=True)  25.3 us
    all_gather x1, waiting for transfers between devices, per_device(): kv_full = lax.all_gather(kv_part, 'seq', axis=1, tiled=True)  16.2 us
    all_to_all x1, blocking collectives, per_device(): lax.all_to_all(back_out, 'doc', split_axis=0, concat_axis=0, tiled=True)  13.2 us
  transfers between devices with their start and end apart: 7, of which 7 were waited for; matrix products, arithmetic and copies ran while one was open for 3% of the time, Pallas kernels for 0%

commit v1 on v0

--- a/solution.py
+++ b/solution.py
@@ -5,6 +5,11 @@
 from jax.sharding import PartitionSpec as P
 
 EPS = 1e-05
+
+
+def swapped_in(x, name, dim):
+    sent = jnp.stack([x] * lax.axis_size(name))
+    return jnp.concatenate(lax.all_to_all(sent, name, 0, 0), axis=dim)
 
 
 def cross_core(kv_tiles, query_rows, grad_rows, q_gain, k_gain, key_live, row_live):
@@ -96,7 +101,7 @@
     own_cols = images[0].reshape(slots * tile_rows, images.shape[3])
     partial_value = lax.dot_general(
         own_cols,
-        lax.all_gather(kv_weight, "doc", axis=0, tiled=True),
+        swapped_in(kv_weight, "doc", 0),
         (((1,), (1,)), ((), ())),
         preferred_element_type=jnp.float32,
     )

time: 443 us -> 453 us (1.023)
  blocking collectives: 13.2 us -> 67.2 us
  waiting for transfers between devices: 272 us -> 230 us
    all_to_all x0 -> x1, blocking collectives: none -> 54 us  [swapped_in(): return jnp.concatenate(lax.all_to_all(sent, name, 0, 0), axis=dim)]
    all_gather x1 -> x0, waiting for transfers between devices: 41.2 us -> none  [per_device(): lax.all_gather(kv_weight, 'doc', axis=0, tiled=True)]
  transfers between devices with their start and end apart: 7 -> 6, of which waited for: 7 -> 6; matrix products, arithmetic and copies ran while one was open for 3% -> 3% of each run, Pallas kernels for 0% -> 0%
where the time goes in v1:
time: 453 us; the launch traced here: 452 us
  waiting for transfers between devices  230 us (51%)
  matrix products  94.5 us (21%)
  blocking collectives  67.2 us (15%)
  local copies, waits for them, and re-layouts  21.9 us (5%)
  other arithmetic  20.7 us (5%)
  between operations  14 us (3%)
    psum x1, waiting for transfers between devices, per_device(): lax.psum(weight_part.astype(jnp.bfloat16), 'doc').astype(jnp.float32)  77.2 us
    all_to_all x1, blocking collectives, swapped_in(): return jnp.concatenate(lax.all_to_all(sent, name, 0, 0), axis=dim)  54 us
    psum x1, waiting for transfers between devices, per_device(): grad_sum = lax.psum(grad_kv.astype(jnp.bfloat16), 'seq').astype(jnp.float32)  51.4 us
    psum x1, waiting for transfers between devices, per_device(): lax.psum(partial_value.astype(jnp.bfloat16), 'seq').astype(jnp.float32)  51.2 us
    dot_general x4, matrix products, one_head(): jnp.einsum('tgl,tgd->ld', grad_low, query_head, preferred_element_type=jn...  39.3 us
    all_gather x1, waiting for transfers between devices, per_device(): grad_full = lax.all_gather(returned, 'seq', axis=1, tiled=True)  25.3 us
    all_gather x1, waiting for transfers between devices, per_device(): kv_full = lax.all_gather(kv_part, 'seq', axis=1, tiled=True)  16.1 us
    all_to_all x1, blocking collectives, per_device(): lax.all_to_all(back_out, 'doc', split_axis=0, concat_axis=0, tiled=True)  13.2 us
  transfers between devices with their start and end apart: 6, of which 6 were waited for; matrix products, arithmetic and copies ran while one was open for 3% of the time, Pallas kernels for 0%

profile of v1, /device:TPU:0, one launch (start us, length us, event | category | flops | bytes accessed | tf_op | source)
XLA Modules:
  0.0 452.3 jit_solution(15733421726068148780)
XLA Ops:
  7.2 1.7 stack.2
  8.9 54.0 %all_to_all.15 = bf16[8,128,2048]{2,1,0:T(8,128)(2,1)S(1)} all-to-all(bf16[8,128,2048]{2,1,0:T(8,128)(2,1)S(1)} %stack.2), channel_id=1, replica_groups=mesh['doc'=8,'seq'=4] {'doc'}, dimensions={0} | all-to-all | bytes 8388608 | tf_op jit(solution)/shard_map/all_to_all | solution.py:12
  63.0 3.3 fusion.63
  66.5 51.2 %all-reduce.4.cloned.1.call-done = bf16[4,128,1024]{2,1,0:T(8,128)(2,1)} async-done(((bf16[4,128,1024]{2,1,0:T(8,128)(2,1)}), bf16[4,128,1024]{2,1,0:T(8,128)(2,1)}) %all-reduce.4.cloned.1.call-update) | async-done | bytes 1048592 | tf_op jit(solution)/shard_map/psum | solution.py:110
  117.8 1.0 convert_convert_fusion.1
  119.2 1.1 copy.35
  120.3 3.7 all-to-all-start.1
  124.0 0.6 dynamic_slice.36
  124.7 0.6 iota_compare_fusion.2
  125.3 8.4 %all-to-all-done.1 = bf16[8,32,1024]{2,1,0:T(8,128)(2,1)S(1)} async-done(((bf16[8,32,1024]{2,1,0:T(8,128)(2,1)}), bf16[8,32,1024]{2,1,0:T(8,128)(2,1)S(1)}, u32[]{:S(2)}, u32[]{:S(2)}) %all-to-all-start.1) | async-done | bytes 524320 | tf_op jit(solution)/shard_map/all_to_all | solution.py:120
  133.6 1.2 convolution_convert_fusion.4
  135.1 0.7 dynamic_slice.39
  135.7 2.3 copy.40
  138.0 1.6 copy.33
  139.7 0.7 fusion.83
  140.6 2.3 multiply_bitcast_fusion
  142.9 1.4 fusion.66
  144.3 16.1 %all-gather.3.cloned.1.call-done = bf16[4,128,1024]{2,0,1:T(4,128)(2,1)} async-done(((bf16[4,32,1024]{2,0,1:T(4,128)(2,1)}), bf16[4,128,1024]{2,0,1:T(4,128)(2,1)}) %all-gather.3.cloned.1.call-update) | async-done | bytes 1048592 | tf_op jit(solution)/shard_map/all_gather | solution.py:128
  160.4 1.5 copy.37
  161.9 1.3 fusion.86
  163.3 1.6 copy.38
  165.0 2.1 copy.39
  167.0 1.0 fusion.70
  168.0 87.8 %while.15 = (s32[]{:T(128)}, bf16[4,128,8,128]{3,1,2,0:T(8,128)(2,1)}, f32[4,512,128]{1,2,0:T(8,128)}, bf16[4,512,128]{2,1,0:T(8,128)(2,1)}, bf16[4,128,8,128]{1...) while((s32[]{:T(128)}, ...), condition=%wide.region_6.7_spmd.clone, body=%wide.region_3.6_spmd.clone.sunk | while | flops 682891136 | bytes 27433116 | solution.py:67
  168.5 2.8 fusion.113
  171.3 2.7 fusion.115
  174.1 9.8 %fusion.116 = f32[4,512,128]{1,2,0:T(8,128)} fusion(f32[4,512,128]{1,2,0:T(8,128)} %get-tuple-element.222, s32[]{:T(128)} %get-tuple-element.220, f32[128,8,512]{2,0,1:T(8,128)} %fusion.115, bf16[4,128,8,128]{1,3,2,0:T(8,128)(2,1)} %get-tuple-element.236, f32[128,8,512]{2,0,1:T(8,128)} %get-tuple-element.206, f32[128,8]{0,1:T(8,128)S(1)} %get-tuple-element.207, ...), kind=kOutput, calls=%fused_computation.13.clone.1 | convolution fusion | flops 139986432 | bytes 8926208 | tf_op jit(solution)/shard_map/while/body/eval_jaxpr/tgl,tgd->ld/dot_general | solution.py:53
  183.9 3.1 fusion.117
  187.0 0.7 compare_convert_fusion.3
  187.7 2.2 fusion.114
  190.5 2.8 fusion.113
  193.3 2.7 fusion.115
  196.0 9.8 %fusion.116 = f32[4,512,128]{1,2,0:T(8,128)} fusion(f32[4,512,128]{1,2,0:T(8,128)} %get-tuple-element.222, s32[]{:T(128)} %get-tuple-element.220, f32[128,8,512]{2,0,1:T(8,128)} %fusion.115, bf16[4,128,8,128]{1,3,2,0:T(8,128)(2,1)} %get-tuple-element.236, f32[128,8,512]{2,0,1:T(8,128)} %get-tuple-element.206, f32[128,8]{0,1:T(8,128)S(1)} %get-tuple-element.207, ...), kind=kOutput, calls=%fused_computation.13.clone.1 | convolution fusion | flops 139986432 | bytes 8926208 | tf_op jit(solution)/shard_map/while/body/eval_jaxpr/tgl,tgd->ld/dot_general | solution.py:53
  205.8 3.1 fusion.117
  208.9 0.7 compare_convert_fusion.3
  209.6 2.2 fusion.114
  212.4 2.8 fusion.113
  215.2 2.7 fusion.115
  218.0 9.8 %fusion.116 = f32[4,512,128]{1,2,0:T(8,128)} fusion(f32[4,512,128]{1,2,0:T(8,128)} %get-tuple-element.222, s32[]{:T(128)} %get-tuple-element.220, f32[128,8,512]{2,0,1:T(8,128)} %fusion.115, bf16[4,128,8,128]{1,3,2,0:T(8,128)(2,1)} %get-tuple-element.236, f32[128,8,512]{2,0,1:T(8,128)} %get-tuple-element.206, f32[128,8]{0,1:T(8,128)S(1)} %get-tuple-element.207, ...), kind=kOutput, calls=%fused_computation.13.clone.1 | convolution fusion | flops 139986432 | bytes 8926208 | tf_op jit(solution)/shard_map/while/body/eval_jaxpr/tgl,tgd->ld/dot_general | solution.py:53
  227.8 3.1 fusion.117
  230.9 0.7 compare_convert_fusion.3
  231.6 2.2 fusion.114
  234.4 2.8 fusion.113
  237.2 2.7 fusion.115
  239.9 9.8 %fusion.116 = f32[4,512,128]{1,2,0:T(8,128)} fusion(f32[4,512,128]{1,2,0:T(8,128)} %get-tuple-element.222, s32[]{:T(128)} %get-tuple-element.220, f32[128,8,512]{2,0,1:T(8,128)} %fusion.115, bf16[4,128,8,128]{1,3,2,0:T(8,128)(2,1)} %get-tuple-element.236, f32[128,8,512]{2,0,1:T(8,128)} %get-tuple-element.206, f32[128,8]{0,1:T(8,128)S(1)} %get-tuple-element.207, ...), kind=kOutput, calls=%fused_computation.13.clone.1 | convolution fusion | flops 139986432 | bytes 8926208 | tf_op jit(solution)/shard_map/while/body/eval_jaxpr/tgl,tgd->ld/dot_general | solution.py:53
  249.7 3.1 fusion.117
  252.8 0.7 compare_convert_fusion.3
  253.5 2.2 fusion.114
  255.8 1.5 fusion.69
  257.3 1.1 fusion.68
  258.4 1.2 reshape.93
  259.6 1.2 copy.49
  261.8 2.5 pad_maximum_fusion
  264.4 51.4 %all-reduce.6.cloned.1.call-done = bf16[4,128,1024]{2,0,1:T(4,128)(2,1)} async-done(((bf16[4,128,1024]{2,0,1:T(4,128)(2,1)}), bf16[4,128,1024]{2,0,1:T(4,128)(2,1)}) %all-reduce.6.cloned.1.call-update) | async-done | bytes 1048592 | tf_op jit(solution)/shard_map/psum | solution.py:146
  315.8 1.4 convolution_convert_fusion.1
  317.4 13.2 %all_to_all.16 = bf16[8,32,1024]{2,1,0:T(8,128)(2,1)S(1)} all-to-all(bf16[8,32,1024]{2,1,0:T(8,128)(2,1)S(1)} %copy.51), channel_id=1, replica_groups=mesh['doc'=8,'seq'=4] {'doc'}, dimensions={0} | all-to-all | bytes 1048576 | tf_op jit(solution)/shard_map/all_to_all | solution.py:152
  330.6 1.1 convolution_convert_fusion.3
  332.0 25.3 %all-gather.5.cloned.1.call-done = bf16[4,128,1024]{2,0,1:T(4,128)(2,1)} async-done(((bf16[4,32,1024]{2,0,1:T(4,128)(2,1)}), bf16[4,128,1024]{2,0,1:T(4,128)(2,1)}) %all-gather.5.cloned.1.call-update) | async-done | bytes 1048592 | tf_op jit(solution)/shard_map/all_gather | solution.py:156
  357.4 1.5 copy.53
  358.9 4.3 convolution_convert_fusion
  363.3 1.9 copy.45
  365.2 1.3 broadcast_in_dim_reshape.3
  366.5 77.2 %all-reduce.8.cloned.1.call-done = bf16[1024,2048]{1,0:T(8,128)(2,1)} async-done(((bf16[1024,2048]{1,0:T(8,128)(2,1)}), bf16[1024,2048]{1,0:T(8,128)(2,1)}) %all-reduce.8.cloned.1.call-update) | async-done | bytes 4194320 | tf_op jit(solution)/shard_map/psum | solution.py:162
  443.6 2.1 dynamic-slice_convert_fusion
  (55 shorter events, 5.4 us)
Async XLA Ops:
  7.2 55.8 %copy-start = (bf16[1,4,128,2048]{3,2,1,0:T(8,128)(2,1)S(1)}, bf16[1,4,128,2048]{3,2,1,0:T(8,128)(2,1)}, u32[]{:S(2)}) copy-start(bf16[1,4,128,2048]{3,2,1,0:T(8,128)(2,1)} %param.12) | copy-start | bytes 6291460
  7.2 110.6 %all-reduce.4.cloned.1.call-start = ((), (), s32[]{:S(2)}) async-start(), calls=%async_computation.3 | async-start | bytes 2097152 | tf_op jit(solution)/shard_map/psum | solution.py:110
  63.0 3.4 copy-start.5
  66.3 57.7 %copy-start.8 = (s32[8]{0:T(128)S(1)}, s32[8]{0:T(128)}, u32[]{:S(2)}) copy-start(s32[8]{0:T(128)} %param.18) | copy-start | bytes 100
  66.3 58.2 %copy-start.6 = (s32[8,4]{0,1:T(4,128)S(1)}, s32[8,4]{0,1:T(4,128)}, u32[]{:S(2)}) copy-start(s32[8,4]{0,1:T(4,128)} %param.20) | copy-start | bytes 388
  118.7 16.3 %copy-start.9 = (s32[8]{0:T(128)S(1)}, s32[8]{0:T(128)}, u32[]{:S(2)}) copy-start(s32[8]{0:T(128)} %param.21) | copy-start | bytes 100
  120.3 13.4 %all-to-all-start.1 = ((bf16[8,32,1024]{2,1,0:T(8,128)(2,1)}), bf16[8,32,1024]{2,1,0:T(8,128)(2,1)S(1)}, u32[]{:S(2)}, u32[]{:S(2)}) async-start(bf16[8,32,1024]{2,1,0:T(8,128)(2,1)} %copy.35), calls=%async_computation.1 | async-start | bytes 1048576 | tf_op jit(solution)/shard_map/all_to_all | solution.py:120
  123.9 36.5 %all-gather.3.cloned.1.call-start = ((), (), s32[]{:S(2)}) async-start(), calls=%async_computation.4 | async-start | bytes 1310720 | tf_op jit(solution)/shard_map/all_gather | solution.py:128
  134.8 181.0 %all-reduce.6.cloned.1.call-start = ((), (), s32[]{:S(2)}) async-start(), calls=%async_computation.5 | async-start | bytes 2097152 | tf_op jit(solution)/shard_map/psum | solution.py:146
  139.6 3.2 copy-start.7
  163.3 3.8 copy-start.4
  183.9 3.8 copy-start.1
  205.8 3.8 copy-start.1
  227.8 3.8 copy-start.1
  249.7 3.8 copy-start.1
  255.8 1.5 copy-start.2
  258.4 2.4 copy-start.3
  264.4 93.0 %all-gather.5.cloned.1.call-start = ((), (), s32[]{:S(2)}) async-start(), calls=%async_computation.6 | async-start | bytes 1310720 | tf_op jit(solution)/shard_map/all_gather | solution.py:156
  331.8 111.8 %all-reduce.8.cloned.1.call-start = ((), (), s32[]{:S(2)}) async-start(), calls=%async_computation.7 | async-start | bytes 8388608 | tf_op jit(solution)/shard_map/psum | solution.py:162
Sparse Core Ops, SparseCore 0:
  66.5 51.2 all-reduce.3
  134.9 25.4 all-gather.2
  264.5 51.2 all-reduce.5
  331.9 25.4 all-gather.4
  363.4 80.1 all-reduce.7
